TPU v7x, 128 devices: a whole 4x4x4 slice. The times are simulated.
128 devices in a mesh: vec: 8 (over y, z_lo), gz: 16 (over x, z_hi, core).
Axes of the slice: x: 4, y: 4, z: 4 (z_hi: 2, z_lo: 2; z = z_hi * 2 + z_lo), core: 2. Of those that a mesh axis runs over, the one named last changes fastest.
Arguments:
- vectors: bfloat16 [1024, 3, 2, 8192], P('vec', None, None, 'gz'), may hold values from -6 to 6
- links: float32 [3, 3, 3, 2, 8192], P(None, None, None, None, 'gz'), may hold values from -4 to 4
- dirs: int32 [6], replicated, may hold values from 0 to 5, each once
- moms: int32 [2, 3], replicated, may hold values from -2 to 2
Outputs:
- elementals: float32 [6, 2, 2, 1024, 1024], P(None, None, None, ('vec', 'gz'))
Inputs may be any that keep to these rules, and one draw needn't show every extreme that they name: `dirs`: each of the six directions appears exactly once.
All inputs are finite; a program needn't handle non-finite values.
Results may differ from a plain program's by a relative error of at most 0.0039.
Values may be sent and summed in bfloat16 or wider, within the bound.
A program may use at most 192 MiB of HBM per device.

v0:
```python
import math
import jax
import jax.numpy as jnp
from jax import lax
from jax.sharding import PartitionSpec as P

LX = 32
LY = 8


def from_behind(shard, axis, by):
    peers = lax.axis_size(axis)
    return lax.ppermute(shard, axis, [(i, (i + by) % peers) for i in range(peers)])


def extended_2(cells, sides, width):
    for axis, dim in sides:
        count = lax.axis_size(axis)
        head = lax.slice_in_dim(cells, 0, width, axis=dim)
        tail = lax.slice_in_dim(cells, cells.shape[dim] - width, cells.shape[dim], axis=dim)
        cells = jnp.concatenate(
            [
                lax.ppermute(tail, axis, [(i, (i + 1) % count) for i in range(count)]),
                cells,
                lax.ppermute(head, axis, [((i + 1) % count, i) for i in range(count)]),
            ],
            axis=dim,
        )
    return cells


def split_up(shard, dim, peers):
    before, after = (shard.shape[:dim], shard.shape[dim + 1 :])
    return jnp.moveaxis(shard.reshape(*before, peers, -1, *after), dim, 0)


def sum_at_owner(shard, axis, dim):
    blocks = split_up(shard, dim, lax.axis_size(axis))
    arrived = lax.all_to_all(blocks, axis, split_axis=0, concat_axis=0, tiled=True)
    return arrived.sum(axis=0)


def colour_apply(link_real, link_imag, vec_real, vec_imag):
    out_real = jnp.float32(0.0)
    out_imag = jnp.float32(0.0)
    for column in range(3):
        left_real = link_real[None, :, column]
        left_imag = link_imag[None, :, column]
        right_real = vec_real[:, None, column].astype(jnp.float32)
        right_imag = vec_imag[:, None, column].astype(jnp.float32)
        out_real = out_real + left_real * right_real - left_imag * right_imag
        out_imag = out_imag + left_real * right_imag + left_imag * right_real
    return (out_real, out_imag)


def neighbour(field, stride, extent, position, forward):
    if forward:
        inside = jnp.roll(field, -stride, axis=-1)
        beside_all = jnp.roll(field, (extent - 1) * stride, axis=-1)
        return jnp.where(position == extent - 1, beside_all, inside)
    inside = jnp.roll(field, stride, axis=-1)
    beside_all = jnp.roll(field, -(extent - 1) * stride, axis=-1)
    return jnp.where(position == 0, beside_all, inside)


def displace(extended, links, lower_links, direction, plane, x_index, y_index):
    sites = links.shape[-1]
    axis_index = direction % 3
    link = links[axis_index]
    if direction < 3:
        if axis_index == 0:
            moved = neighbour(extended[..., plane : plane + sites], 1, LX, x_index, True)
        elif axis_index == 1:
            moved = neighbour(extended[..., plane : plane + sites], LX, LY, y_index, True)
        else:
            moved = extended[..., 2 * plane : 2 * plane + sites]
        link_real = link[:, :, 0]
        link_imag = link[:, :, 1]
    else:
        if axis_index == 0:
            moved = neighbour(extended[..., plane : plane + sites], 1, LX, x_index, False)
            behind = neighbour(link, 1, LX, x_index, False)
        elif axis_index == 1:
            moved = neighbour(extended[..., plane : plane + sites], LX, LY, y_index, False)
            behind = neighbour(link, LX, LY, y_index, False)
        else:
            moved = extended[..., 0:sites]
            behind = jnp.concatenate((lower_links, link), axis=-1)[..., 0:sites]
        link_real = jnp.swapaxes(behind[:, :, 0], 0, 1)
        link_imag = -jnp.swapaxes(behind[:, :, 1], 0, 1)
    disp_real, disp_imag = colour_apply(link_real, link_imag, moved[:, :, 0], moved[:, :, 1])
    return jnp.stack((disp_real.astype(jnp.bfloat16), disp_imag.astype(jnp.bfloat16)), axis=2)


def on_device(vectors, links, dirs, moms):
    sites = vectors.shape[-1]
    plane = LY * LX
    depth = sites // plane
    shards = lax.axis_size("gz")
    flat = jnp.arange(sites, dtype=jnp.int32)
    x_index = flat % LX
    y_index = flat // LX % LY
    z_index = lax.axis_index("gz") * depth + flat // plane
    lower_links = from_behind(links[2, :, :, :, sites - plane :], "gz", 1)
    gathered = lax.all_gather(vectors, "vec", axis=0, tiled=True)
    extended = extended_2(gathered, (("gz", 3),), plane)
    momenta = moms.astype(jnp.float32)
    theta = (
        momenta[:, 0, None] * x_index.astype(jnp.float32) / LX
        + momenta[:, 1, None] * y_index.astype(jnp.float32) / LY
        + momenta[:, 2, None] * z_index.astype(jnp.float32) / (depth * shards)
    ) * (2.0 * math.pi)
    cosine = jnp.cos(theta)[:, None, None]
    sine = jnp.sin(theta)[:, None, None]
    own_f = vectors.astype(jnp.float32)
    real_part = own_f[:, :, 0][None]
    imag_part = own_f[:, :, 1][None]
    phased_real = (cosine * real_part - sine * imag_part).astype(jnp.bfloat16)
    phased_imag = (sine * real_part + cosine * imag_part).astype(jnp.bfloat16)
    left_side = jnp.stack(
        (
            jnp.stack((phased_real, phased_imag), axis=3),
            jnp.stack((-phased_imag, phased_real), axis=3),
        ),
        axis=0,
    )
    terms = []
    for direction in range(6):
        displaced = displace(extended, links, lower_links, direction, plane, x_index, y_index)
        product = jnp.einsum(
            "qpicrs,jcrs->pqij", left_side, displaced, preferred_element_type=jnp.float32
        )
        terms.append(sum_at_owner(product, "gz", 2))
    stacked = jnp.stack(terms, axis=0)
    select = (dirs[:, None] == jnp.arange(6, dtype=jnp.int32)[None, :]).astype(jnp.float32)
    chosen = jnp.einsum("dk,kpqij->dpqij", select, stacked, precision=lax.Precision.HIGHEST)
    return chosen * (1.0 / math.sqrt(3.0 * sites * shards))


def solution(mesh):
    placed = (P("vec", None, None, "gz"), P(None, None, None, None, "gz"), P(), P())
    return jax.shard_map(
        on_device,
        mesh=mesh,
        in_specs=placed,
        out_specs=P(None, None, None, ("vec", "gz"), None),
        check_vma=False,
    )
```

profile of v0, /device:TPU:40, one launch (start us, length us, event | category | flops | bytes accessed | tf_op | source)
XLA Modules:
  0.0 507.7 jit_solution(9093775337054759167)
XLA Ops:
  21.5 120.3 %all-gather.2.cloned.1.call-done = bf16[1024,3,2,512]{3,0,2,1:T(8,128)(2,1)} async-done(((bf16[128,3,2,512]{3,0,2,1:T(8,128)(2,1)}), bf16[1024,3,2,512]{3,0,2,1:T(8,128)(2,1)}) %all-gather.2.cloned.1.call-update) | async-done | bytes 6291472 | tf_op jit(solution)/shard_map/all_gather | solution.py:105
  141.8 7.9 %fusion.92 = (bf16[1024,3,2,481]{3,0,2,1:T(8,128)(2,1)S(1)}, bf16[1024,3,2,481]{3,0,2,1:T(8,128)(2,1)S(1)}) fusion(bf16[1024,3,2,512]{3,0,2,1:T(8,128)(2,1)} %all-gather.2.cloned.1.call-done), kind=kLoop, calls=%fused_computation.256 | loop fusion | bytes 23642112 | tf_op jit(solution)/shard_map/jit(_roll_static)/slice | solution.py:62
  154.0 5.0 fusion.91
  159.0 17.8 %maximum_select_fusion = (bf16[1024,3,2,512]{3,0,2,1:T(8,128)(2,1)}, bf16[1024,3,2,512]{3,0,2,1:T(8,128)(2,1)}) fusion(bf16[1024,3,2,481]{3,0,2,1:T(8,128)(2,1)S(1)} %get-tuple-element.49, bf16[1024,3,2,31]{3,0,2,1:T(8,128)(2,1)} %get-tuple-element.51, bf16[1024,3,2,1]{3,0,2,1:T(8,128)(2,1)} %get-tuple-element.45, ...), kind=kLoop, calls=%fused_computation | loop fusion | flops 56623104 | bytes 37749760 | tf_op jit(solution)/shard_map/jit(_where)/select_n | solution.py:60
  191.5 6.5 %all-to-all-start = ((f32[16,2,2,8,1024]{4,3,1,2,0:T(8,128)}), f32[16,2,2,8,1024]{4,3,1,2,0:T(8,128)}, u32[]{:S(2)}, u32[]{:S(2)}) async-start(f32[16,2,2,8,1024]{4,3,1,2,0:T(8,128)} %bitcast.488), calls=%async_computation | async-start | bytes 4194304 | tf_op jit(solution)/shard_map/all_to_all | solution.py:39
  198.0 10.2 %fusion.88 = (bf16[1024,3,2,288]{3,0,2,1:T(8,128)(2,1)}, bf16[1024,3,2,288]{3,0,2,1:T(8,128)(2,1)}) fusion(bf16[1024,3,2,512]{3,0,2,1:T(8,128)(2,1)} %all-gather.2.cloned.1.call-done), kind=kLoop, calls=%fused_computation.252 | loop fusion | bytes 14155776 | tf_op jit(solution)/shard_map/jit(_roll_static)/slice | solution.py:62
  214.5 6.4 %fusion.87 = (bf16[1024,3,2,480]{3,0,2,1:T(8,128)(2,1)}, bf16[1024,3,2,480]{3,0,2,1:T(8,128)(2,1)}) fusion(bf16[1024,3,2,512]{3,0,2,1:T(8,128)(2,1)S(1)} %bitcast.481), kind=kLoop, calls=%fused_computation.251 | loop fusion | bytes 23592960 | tf_op jit(solution)/shard_map/jit(_roll_static)/slice | solution.py:61
  221.0 17.1 %maximum_select_fusion.1 = (bf16[1024,3,2,512]{3,0,2,1:T(8,128)(2,1)}, bf16[1024,3,2,512]{3,0,2,1:T(8,128)(2,1)S(1)}) fusion(bf16[1024,3,2,288]{3,0,2,1:T(8,128)(2,1)} %get-tuple-element.39, bf16[1024,3,2,224]{3,0,2,1:T(8,128)(2,1)} %get-tuple-element.41, bf16[1024,3,2,32]{3,0,2,1:T(8,128)(2,1)} %get-tuple-element.35, ...), kind=kLoop, calls=%fused_computation.5 | loop fusion | flops 56623104 | bytes 37749760 | tf_op jit(solution)/shard_map/jit(_where)/select_n | solution.py:60
  242.5 5.3 %subtract_convert_fusion.4 = (bf16[1024,3,1,512]{3,0,2,1:T(8,128)(2,1)S(1)}, bf16[1024,3,1,512]{3,0,2,1:T(8,128)(2,1)S(1)}) fusion(f32[1024,512]{1,0:T(8,128)S(1)} %get-tuple-element.84, f32[3,512]{1,0:T(4,128)S(1)} %bitcast.513, f32[1024,512]{1,0:T(8,128)S(1)} %get-tuple-element.81, f32[3,512]{1,0:T(4,128)S(1)} %bitcast.514, ...), kind=kLoop, calls=%fused_computation.37 | loop fusion | flops 37748736 | bytes 18911232 | tf_op jit(solution)/shard_map/convert_element_type | solution.py:92
  277.9 5.4 %all-to-all-start.1 = ((f32[16,2,2,8,1024]{4,3,1,2,0:T(8,128)}), f32[16,2,2,8,1024]{4,3,1,2,0:T(8,128)}, u32[]{:S(2)}, u32[]{:S(2)}) async-start(f32[16,2,2,8,1024]{4,3,1,2,0:T(8,128)} %bitcast.489), calls=%async_computation.1 | async-start | bytes 4194304 | tf_op jit(solution)/shard_map/all_to_all | solution.py:39
  287.1 6.3 %subtract_convert_fusion.1 = (bf16[1024,3,1,512]{3,0,2,1:T(8,128)(2,1)}, bf16[1024,3,1,512]{3,0,2,1:T(8,128)(2,1)}) fusion(f32[1024,512]{1,0:T(8,128)S(1)} %get-tuple-element.66, f32[3,512]{1,0:T(4,128)S(1)} %copy-done.18, f32[1024,512]{1,0:T(8,128)S(1)} %get-tuple-element.63, f32[3,512]{1,0:T(4,128)S(1)} %copy-done.27, ...), kind=kLoop, calls=%fused_computation.31 | loop fusion | flops 37748736 | bytes 18911232 | tf_op jit(solution)/shard_map/convert_element_type | solution.py:92
  293.4 59.5 %all-to-all-done.1 = f32[16,2,2,8,1024]{4,3,1,2,0:T(8,128)} async-done(((f32[16,2,2,8,1024]{4,3,1,2,0:T(8,128)}), f32[16,2,2,8,1024]{4,3,1,2,0:T(8,128)}, u32[]{:S(2)}, u32[]{:S(2)}) %all-to-all-start.1) | async-done | bytes 2097184 | tf_op jit(solution)/shard_map/all_to_all | solution.py:39
  352.9 6.1 %all-to-all-start.3 = ((f32[16,2,2,8,1024]{4,3,1,2,0:T(8,128)}), f32[16,2,2,8,1024]{4,3,1,2,0:T(8,128)}, u32[]{:S(2)}, u32[]{:S(2)}) async-start(f32[16,2,2,8,1024]{4,3,1,2,0:T(8,128)} %bitcast.450), calls=%async_computation.3 | async-start | bytes 4194304 | tf_op jit(solution)/shard_map/all_to_all | solution.py:39
  359.0 7.3 %fusion.19 = f32[2,2,16,8,1024]{4,3,2,0,1:T(8,128)S(1)} fusion(bf16[1024,3,1,512]{3,0,2,1:T(8,128)(2,1)} %get-tuple-element.15, bf16[1024,3,1,512]{3,0,2,1:T(8,128)(2,1)} %get-tuple-element.14, bf16[1,2,128,3,2,512]{5,2,4,3,1,0:T(8,128)(2,1)} %get-tuple-element.95, bf16[1,2,128,3,2,512]{5,2,4,3,1,0:T(8,128)(2,1)} %get-tuple-element.94), kind=kOutput, calls=%fused_computation.60 | convolution fusion | flops 3240099840 | bytes 11534336 | tf_op jit(solution)/shard_map/qpicrs,jcrs->pqij/dot_general | solution.py:130
  371.7 6.1 %constant_dynamic-update-slice_fusion.2 = (bf16[1024,3,2,768]{3,0,2,1:T(8,128)(2,1)}, bf16[1024,3,2,768]{3,0,2,1:T(8,128)(2,1)}) fusion(bf16[1024,3,2,768]{3,0,2,1:T(8,128)(2,1)} %constant_dynamic-update-slice_fusion.3, bf16[1024,3,2,512]{3,0,2,1:T(8,128)(2,1)S(1)} %bitcast.483), kind=kLoop, calls=%fused_computation.169 | loop fusion | bytes 18874368 | tf_op jit(solution)/shard_map/concatenate | solution.py:21
  385.5 5.1 fusion.46
  390.5 7.4 %all-to-all-start.4 = ((f32[16,2,2,8,1024]{4,3,1,2,0:T(8,128)}), f32[16,2,2,8,1024]{4,3,1,2,0:T(8,128)S(1)}, u32[]{:S(2)}, u32[]{:S(2)}) async-start(f32[16,2,2,8,1024]{4,3,1,2,0:T(8,128)} %bitcast.490), calls=%async_computation.4 | async-start | bytes 4194304 | tf_op jit(solution)/shard_map/all_to_all | solution.py:39
  398.0 8.4 %subtract_convert_fusion.3 = (bf16[1024,3,1,512]{3,0,2,1:T(8,128)(2,1)S(1)}, bf16[1024,3,1,512]{3,0,2,1:T(8,128)(2,1)S(1)}) fusion(f32[1024,512]{1,0:T(8,128)} %get-tuple-element.78, f32[3,512]{1,0:T(4,128)S(1)} %bitcast.507, f32[1024,512]{1,0:T(8,128)} %get-tuple-element.160, f32[3,512]{1,0:T(4,128)S(1)} %bitcast.508, f32[1024,512]{1,0:T(8,128)} %get-tuple-element.79, ...), kind=kLoop, calls=%fused_computation.35 | loop fusion | flops 37748736 | bytes 18911232 | tf_op jit(solution)/shard_map/convert_element_type | solution.py:92
  412.0 5.1 %fusion.28 = (f32[1024,512]{1,0:T(8,128)}, f32[1024,512]{1,0:T(8,128)}, f32[1024,512]{1,0:T(8,128)}, f32[1024,512]{1,0:T(8,128)}, f32[1024,512]{1,0:T(8,128)}, /*index=5*/f32[1024,512]{1,0:T(8,128)}) fusion(bf16[1024,3,512]{2,0,1:T(8,128)(2,1)S(1)} %get-tuple-element.25, bf16[1024,3,512]{2,0,1:T(8,128)(2,1)S(1)} %get-tuple-element.24), kind=kLoop, calls=%fused_computation.79 | loop fusion | flops 3145728 | bytes 18874368 | tf_op jit(solution)/shard_map/mul | solution.py:51
  417.1 10.0 %all-to-all-done.4 = f32[16,2,2,8,1024]{4,3,1,2,0:T(8,128)S(1)} async-done(((f32[16,2,2,8,1024]{4,3,1,2,0:T(8,128)}), f32[16,2,2,8,1024]{4,3,1,2,0:T(8,128)S(1)}, u32[]{:S(2)}, u32[]{:S(2)}) %all-to-all-start.4) | async-done | bytes 2097184 | tf_op jit(solution)/shard_map/all_to_all | solution.py:39
  432.1 7.8 %subtract_convert_fusion = (bf16[1024,3,1,512]{3,0,2,1:T(8,128)(2,1)S(1)}, bf16[1024,3,1,512]{3,0,2,1:T(8,128)(2,1)S(1)}) fusion(f32[1024,512]{1,0:T(8,128)} %get-tuple-element.60, f32[3,512]{1,0:T(4,128)S(1)} %copy-done.21, f32[1024,512]{1,0:T(8,128)} %get-tuple-element.167, f32[3,512]{1,0:T(4,128)S(1)} %copy-done.24, f32[1024,512]{1,0:T(8,128)} %get-tuple-element.61, ...), kind=kLoop, calls=%fused_computation.29 | loop fusion | flops 37748736 | bytes 18911232 | tf_op jit(solution)/shard_map/convert_element_type | solution.py:92
  444.9 16.4 %all-to-all-done.2 = f32[16,2,2,8,1024]{4,3,1,2,0:T(8,128)} async-done(((f32[16,2,2,8,1024]{4,3,1,2,0:T(8,128)}), f32[16,2,2,8,1024]{4,3,1,2,0:T(8,128)}, u32[]{:S(2)}, u32[]{:S(2)}) %all-to-all-start.2) | async-done | bytes 2097184 | tf_op jit(solution)/shard_map/all_to_all | solution.py:39
  461.3 5.0 all-to-all-start.5
  474.0 21.5 %all-to-all-done.5 = f32[16,2,2,8,1024]{4,3,1,2,0:T(8,128)} async-done(((f32[16,2,2,8,1024]{4,3,1,2,0:T(8,128)}), f32[16,2,2,8,1024]{4,3,1,2,0:T(8,128)}, u32[]{:S(2)}, u32[]{:S(2)}) %all-to-all-start.5) | async-done | bytes 2097184 | tf_op jit(solution)/shard_map/all_to_all | solution.py:39
  (210 shorter events, 119.0 us)
Async XLA Ops:
  6.5 135.2 %all-gather.2.cloned.1.call-start = ((), (), s32[]{:S(2)}) async-start(), calls=%async_computation.6 | async-start | bytes 7077888 | tf_op jit(solution)/shard_map/all_gather | solution.py:105
  9.6 6.8 %collective-permute-start.1 = (f32[3,3,2,256]{3,2,1,0:T(2,128)S(1)}, f32[3,3,2,256]{3,2,1,0:T(2,128)S(1)}, u32[]{:S(2)}, u32[]{:S(2)}) collective-permute-start(f32[3,3,2,256]{3,2,1,0:T(2,128)S(1)} %slice_bitcast_fusion.53), channel_id=1, source_target_pairs={{0,1},{1,2},{2,3},{3,4},{4,5},{5,6},{6,7},{7,8},{8,9},{9,10},{10,1... | collective-permute-start | bytes 55304 | tf_op jit(solution)/shard_map/ppermute | solution.py:13
  191.5 16.7 %slice-start = ((s8[6291456]{0:T(1024)(128)(4,1)}), s8[2097152]{0:T(1024)(128)(4,1)S(1)}, s32[]{:S(2)}) async-start(s8[6291456]{0:T(1024)(128)(4,1)} %bitcast.480), calls=%async_computation.7 | async-start | bytes 4194304
  191.5 86.4 %all-to-all-start = ((f32[16,2,2,8,1024]{4,3,1,2,0:T(8,128)}), f32[16,2,2,8,1024]{4,3,1,2,0:T(8,128)}, u32[]{:S(2)}, u32[]{:S(2)}) async-start(f32[16,2,2,8,1024]{4,3,1,2,0:T(8,128)} %bitcast.488), calls=%async_computation | async-start | bytes 4194304 | tf_op jit(solution)/shard_map/all_to_all | solution.py:39
  257.5 110.3 %collective-permute-start.2 = (bf16[1024,3,2,256]{3,0,2,1:T(8,128)(2,1)}, bf16[1024,3,2,256]{3,0,2,1:T(8,128)(2,1)}, u32[]{:S(2)}, u32[]{:S(2)}) collective-permute-start(bf16[1024,3,2,256]{3,0,2,1:T(8,128)(2,1)} %get-tuple-element.30), channel_id=1, source_target_pairs={{0,1},{1,2},{2,3},{3,4},{4,5},{5,6},{6,7},{7,8},{8,9},{9,10},{10,1... | collective-permute-start | bytes 9437192 | tf_op jit(solution)/shard_map/ppermute | solution.py:23
  258.0 119.8 %collective-permute-start = (bf16[1024,3,2,256]{3,0,2,1:T(8,128)(2,1)}, bf16[1024,3,2,256]{3,0,2,1:T(8,128)(2,1)}, u32[]{:S(2)}, u32[]{:S(2)}) collective-permute-start(bf16[1024,3,2,256]{3,0,2,1:T(8,128)(2,1)} %get-tuple-element.31), channel_id=1, source_target_pairs={{1,0},{2,1},{3,2},{4,3},{5,4},{6,5},{7,6},{8,7},{9,8},{10,9},{11,1... | collective-permute-start | bytes 9437192 | tf_op jit(solution)/shard_map/ppermute | solution.py:25
  277.9 75.0 %all-to-all-start.1 = ((f32[16,2,2,8,1024]{4,3,1,2,0:T(8,128)}), f32[16,2,2,8,1024]{4,3,1,2,0:T(8,128)}, u32[]{:S(2)}, u32[]{:S(2)}) async-start(f32[16,2,2,8,1024]{4,3,1,2,0:T(8,128)} %bitcast.489), calls=%async_computation.1 | async-start | bytes 4194304 | tf_op jit(solution)/shard_map/all_to_all | solution.py:39
  352.9 37.6 %all-to-all-start.3 = ((f32[16,2,2,8,1024]{4,3,1,2,0:T(8,128)}), f32[16,2,2,8,1024]{4,3,1,2,0:T(8,128)}, u32[]{:S(2)}, u32[]{:S(2)}) async-start(f32[16,2,2,8,1024]{4,3,1,2,0:T(8,128)} %bitcast.450), calls=%async_computation.3 | async-start | bytes 4194304 | tf_op jit(solution)/shard_map/all_to_all | solution.py:39
  359.0 12.7 %slice-start.2 = ((s8[6291456]{0:T(1024)(128)(4,1)}), s8[4194304]{0:T(1024)(128)(4,1)S(1)}, s32[]{:S(2)}) async-start(s8[6291456]{0:T(1024)(128)(4,1)} %bitcast.482), calls=%async_computation.9 | async-start | bytes 8388608
  359.0 12.7 %slice-start.3 = ((s8[6291456]{0:T(1024)(128)(4,1)}), s8[2097152]{0:T(1024)(128)(4,1)S(1)}, s32[]{:S(2)}) async-start(s8[6291456]{0:T(1024)(128)(4,1)} %bitcast.482), calls=%async_computation.10 | async-start | bytes 4194304
  385.4 12.5 %copy-start.11 = (f32[3,1,512]{2,0,1:T(4,128)S(1)}, f32[3,1,512]{2,0,1:T(4,128)}, u32[]{:S(2)}) copy-start(f32[3,1,512]{2,0,1:T(4,128)} %copy.137) | copy-start | bytes 18436
  385.4 12.5 %copy-start.12 = (f32[3,1,512]{2,0,1:T(4,128)S(1)}, f32[3,1,512]{2,0,1:T(4,128)}, u32[]{:S(2)}) copy-start(f32[3,1,512]{2,0,1:T(4,128)} %copy.138) | copy-start | bytes 18436
  385.4 12.5 %copy-start.13 = (f32[3,1,512]{2,0,1:T(4,128)S(1)}, f32[3,1,512]{2,0,1:T(4,128)}, u32[]{:S(2)}) copy-start(f32[3,1,512]{2,0,1:T(4,128)} %copy.139) | copy-start | bytes 18436
  390.5 36.5 %all-to-all-start.4 = ((f32[16,2,2,8,1024]{4,3,1,2,0:T(8,128)}), f32[16,2,2,8,1024]{4,3,1,2,0:T(8,128)S(1)}, u32[]{:S(2)}, u32[]{:S(2)}) async-start(f32[16,2,2,8,1024]{4,3,1,2,0:T(8,128)} %bitcast.490), calls=%async_computation.4 | async-start | bytes 4194304 | tf_op jit(solution)/shard_map/all_to_all | solution.py:39
  398.0 13.4 %slice-start.6 = ((s8[9437184]{0:T(1024)(128)(4,1)}), s8[4194304]{0:T(1024)(128)(4,1)S(1)}, s32[]{:S(2)}) async-start(s8[9437184]{0:T(1024)(128)(4,1)} %bitcast.486), calls=%async_computation.13 | async-start | bytes 8388608
  411.9 20.1 %copy-start.20 = (f32[3,512]{1,0:T(4,128)S(1)}, f32[3,512]{1,0:T(4,128)}, u32[]{:S(2)}) copy-start(f32[3,512]{1,0:T(4,128)} %get-tuple-element.116) | copy-start | bytes 18436
  411.9 20.1 %copy-start.21 = (f32[3,512]{1,0:T(4,128)S(1)}, f32[3,512]{1,0:T(4,128)}, u32[]{:S(2)}) copy-start(f32[3,512]{1,0:T(4,128)} %get-tuple-element.117) | copy-start | bytes 18436
  411.9 20.1 %copy-start.22 = (f32[3,512]{1,0:T(4,128)S(1)}, f32[3,512]{1,0:T(4,128)}, u32[]{:S(2)}) copy-start(f32[3,512]{1,0:T(4,128)} %get-tuple-element.118) | copy-start | bytes 18436
  411.9 20.1 %copy-start.23 = (f32[3,512]{1,0:T(4,128)S(1)}, f32[3,512]{1,0:T(4,128)}, u32[]{:S(2)}) copy-start(f32[3,512]{1,0:T(4,128)} %get-tuple-element.113) | copy-start | bytes 18436
  411.9 20.1 %copy-start.24 = (f32[3,512]{1,0:T(4,128)S(1)}, f32[3,512]{1,0:T(4,128)}, u32[]{:S(2)}) copy-start(f32[3,512]{1,0:T(4,128)} %get-tuple-element.114) | copy-start | bytes 18436
  411.9 20.1 %copy-start.25 = (f32[3,512]{1,0:T(4,128)S(1)}, f32[3,512]{1,0:T(4,128)}, u32[]{:S(2)}) copy-start(f32[3,512]{1,0:T(4,128)} %get-tuple-element.115) | copy-start | bytes 18436
  427.1 34.2 %all-to-all-start.2 = ((f32[16,2,2,8,1024]{4,3,1,2,0:T(8,128)}), f32[16,2,2,8,1024]{4,3,1,2,0:T(8,128)}, u32[]{:S(2)}, u32[]{:S(2)}) async-start(f32[16,2,2,8,1024]{4,3,1,2,0:T(8,128)} %bitcast.491), calls=%async_computation.2 | async-start | bytes 4194304 | tf_op jit(solution)/shard_map/all_to_all | solution.py:39
  461.3 34.2 %all-to-all-start.5 = ((f32[16,2,2,8,1024]{4,3,1,2,0:T(8,128)}), f32[16,2,2,8,1024]{4,3,1,2,0:T(8,128)}, u32[]{:S(2)}, u32[]{:S(2)}) async-start(f32[16,2,2,8,1024]{4,3,1,2,0:T(8,128)} %bitcast.492), calls=%async_computation.5 | async-start | bytes 4194304 | tf_op jit(solution)/shard_map/all_to_all | solution.py:39
  469.8 28.8 %copy-start.29 = (s32[6]{0:T(128)S(1)}, s32[6]{0:T(128)}, u32[]{:S(2)}) copy-start(s32[6]{0:T(128)} %param.6) | copy-start | bytes 76
  (25 other events, 149.9 us)
Sparse Core Ops, SparseCore 0:
  9.0 132.7 all-gather.1
where the time goes:
time: 511 us; the launch traced here: 508 us
  waiting for transfers between devices  228 us (45%)
  other arithmetic  106 us (21%)
  local copies, waits for them, and re-layouts  91.6 us (18%)
  starting transfers between devices  40.7 us (8%)
  matrix products  26.5 us (5%)
  between operations  14.8 us (3%)
    all_gather x1, waiting for transfers between devices, on_device(): gathered = lax.all_gather(vectors, 'vec', axis=0, tiled=True)  120 us
    all_to_all x6, waiting for transfers between devices, sum_at_owner(): lax.all_to_all(blocks, axis, split_axis=0, concat_axis=0, tiled=True)  107 us
    convert_element_type x6, other arithmetic, displace(): disp_real.astype(jnp.bfloat16)  37.8 us
    all_to_all x6, starting transfers between devices, sum_at_owner(): lax.all_to_all(blocks, axis, split_axis=0, concat_axis=0, tiled=True)  35.3 us
    select_n x2, other arithmetic, neighbour(): return jnp.where(position == extent - 1, beside_all, inside)  34.9 us
    dot_general x6, matrix products, on_device(): jnp.einsum('qpicrs,jcrs->pqij', left_side, displaced, preferred_element_t...  25.9 us
    slice x8, local copies, waits for them, and re-layouts, neighbour(): beside_all = jnp.roll(field, -(extent - 1) * stride, axis=-1)  24.6 us
    mul x10, other arithmetic, colour_apply(): out_real = out_real + left_real * right_real - left_imag * right_imag  19 us
  transfers between devices with their start and end apart: 10, of which 5 were waited for; matrix products, arithmetic and copies ran while one was open for 33% of the time, Pallas kernels for 0%

commit v1 on v0

--- a/solution.py
+++ b/solution.py
@@ -102,7 +102,9 @@
     y_index = flat // LX % LY
     z_index = lax.axis_index("gz") * depth + flat // plane
     lower_links = from_behind(links[2, :, :, :, sites - plane :], "gz", 1)
-    gathered = lax.all_gather(vectors, "vec", axis=0, tiled=True)
+    gathered = jnp.concatenate(
+        lax.all_to_all(jnp.stack([vectors] * lax.axis_size("vec")), "vec", 0, 0), axis=0
+    )
     extended = extended_2(gathered, (("gz", 3),), plane)
     momenta = moms.astype(jnp.float32)
     theta = (

time: 511 us -> 453 us (0.89)
  the two profiles are of different devices: /device:TPU:40 before, /device:TPU:1 now
where the time goes in v1:
time: 453 us; the launch traced here: 449 us
  waiting for transfers between devices  184 us (41%)
  other arithmetic  113 us (25%)
  local copies, waits for them, and re-layouts  72 us (16%)
  starting transfers between devices  53.9 us (12%)
  matrix products  25.1 us (6%)
    all_to_all x6, waiting for transfers between devices, sum_at_owner(): lax.all_to_all(blocks, axis, split_axis=0, concat_axis=0, tiled=True)  112 us
    ppermute x1, waiting for transfers between devices, from_behind(): lax.ppermute(shard, axis, [(i, (i + by) % peers) for i in range(peers)])  40.7 us
    all_to_all x6, starting transfers between devices, sum_at_owner(): lax.all_to_all(blocks, axis, split_axis=0, concat_axis=0, tiled=True)  40.1 us
    convert_element_type x6, other arithmetic, displace(): disp_real.astype(jnp.bfloat16)  40 us
    select_n x2, other arithmetic, neighbour(): return jnp.where(position == extent - 1, beside_all, inside)  35.1 us
    all_to_all x1, waiting for transfers between devices, on_device(): lax.all_to_all(jnp.stack([vectors] * lax.axis_size('vec')), 'vec', 0, 0)  31.4 us
    dot_general x6, matrix products, on_device(): jnp.einsum('qpicrs,jcrs->pqij', left_side, displaced, preferred_element_t...  24.5 us
    mul x10, other arithmetic, colour_apply(): out_real = out_real + left_real * right_real - left_imag * right_imag  21 us
  transfers between devices with their start and end apart: 10, of which 7 were waited for; matrix products, arithmetic and copies ran while one was open for 28% of the time, Pallas kernels for 0%

profile of v1, /device:TPU:1, one launch (start us, length us, event | category | flops | bytes accessed | tf_op | source)
XLA Modules:
  0.0 449.1 jit_solution(8223257192149292229)
XLA Ops:
  4.7 6.5 %all-to-all-start = ((bf16[8,128,3,2,512]{4,1,2,3,0:T(8,128)(2,1)}), bf16[8,128,3,2,512]{4,1,2,3,0:T(8,128)(2,1)}, u32[]{:S(2)}, u32[]{:S(2)}) async-start(bf16[8,128,3,2,512]{4,1,2,3,0:T(8,128)(2,1)} %stack.38), calls=%async_computation | async-start | bytes 12582912 | tf_op jit(solution)/shard_map/all_to_all | solution.py:106
  21.0 40.7 %collective-permute-done.1 = f32[3,3,2,256]{3,2,1,0:T(2,128)S(1)} collective-permute-done((f32[3,3,2,256]{3,2,1,0:T(2,128)S(1)}, f32[3,3,2,256]{3,2,1,0:T(2,128)S(1)}, u32[]{:S(2)}, u32[]{:S(2)}) %collective-permute-start.1) | collective-permute-done | bytes 18464 | tf_op jit(solution)/shard_map/ppermute | solution.py:13
  66.8 31.4 %all-to-all-done = bf16[8,128,3,2,512]{4,1,2,3,0:T(8,128)(2,1)} async-done(((bf16[8,128,3,2,512]{4,1,2,3,0:T(8,128)(2,1)}), bf16[8,128,3,2,512]{4,1,2,3,0:T(8,128)(2,1)}, u32[]{:S(2)}, u32[]{:S(2)}) %all-to-all-start) | async-done | bytes 6291488 | tf_op jit(solution)/shard_map/all_to_all | solution.py:106
  101.5 7.1 %fusion.94 = (bf16[1024,3,2,481]{3,0,2,1:T(8,128)(2,1)}, bf16[1024,3,2,481]{3,0,2,1:T(8,128)(2,1)}) fusion(bf16[1024,3,2,512]{3,0,2,1:T(8,128)(2,1)S(1)} %bitcast.481), kind=kLoop, calls=%fused_computation.254 | loop fusion | bytes 23642112 | tf_op jit(solution)/shard_map/jit(_roll_static)/slice | solution.py:62
  113.4 6.3 %fusion.93 = (bf16[1024,3,2,511]{3,0,2,1:T(8,128)(2,1)}, bf16[1024,3,2,511]{3,0,2,1:T(8,128)(2,1)}) fusion(bf16[1024,3,2,512]{3,0,2,1:T(8,128)(2,1)S(1)} %bitcast.484), kind=kLoop, calls=%fused_computation.253 | loop fusion | bytes 25116672 | tf_op jit(solution)/shard_map/jit(_roll_static)/slice | solution.py:61
  119.7 6.8 %fusion.90 = (bf16[1024,3,2,288]{3,0,2,1:T(8,128)(2,1)}, bf16[1024,3,2,288]{3,0,2,1:T(8,128)(2,1)}) fusion(bf16[1024,3,2,512]{3,0,2,1:T(8,128)(2,1)S(1)} %bitcast.485), kind=kLoop, calls=%fused_computation.250 | loop fusion | bytes 14155776 | tf_op jit(solution)/shard_map/jit(_roll_static)/slice | solution.py:62
  132.6 6.5 %fusion.89 = (bf16[1024,3,2,480]{3,0,2,1:T(8,128)(2,1)}, bf16[1024,3,2,480]{3,0,2,1:T(8,128)(2,1)}) fusion(bf16[1024,3,2,512]{3,0,2,1:T(8,128)(2,1)S(1)} %bitcast.488), kind=kLoop, calls=%fused_computation.249 | loop fusion | bytes 23592960 | tf_op jit(solution)/shard_map/jit(_roll_static)/slice | solution.py:61
  142.3 18.0 %maximum_select_fusion = (bf16[1024,3,2,512]{3,0,2,1:T(8,128)(2,1)S(1)}, bf16[1024,3,2,512]{3,0,2,1:T(8,128)(2,1)}) fusion(bf16[1024,3,2,481]{3,0,2,1:T(8,128)(2,1)} %get-tuple-element.49, bf16[1024,3,2,31]{3,0,2,1:T(8,128)(2,1)} %get-tuple-element.51, bf16[1024,3,2,1]{3,0,2,1:T(8,128)(2,1)} %get-tuple-element.45, ...), kind=kLoop, calls=%fused_computation | loop fusion | flops 56623104 | bytes 37749760 | tf_op jit(solution)/shard_map/jit(_where)/select_n | solution.py:60
  172.6 9.7 %all-to-all-start.1 = ((f32[16,2,2,8,1024]{4,3,1,2,0:T(8,128)}), f32[16,2,2,8,1024]{4,3,1,2,0:T(8,128)}, u32[]{:S(2)}, u32[]{:S(2)}) async-start(f32[16,2,2,8,1024]{4,3,1,2,0:T(8,128)} %bitcast.499), calls=%async_computation.1 | async-start | bytes 4194304 | tf_op jit(solution)/shard_map/all_to_all | solution.py:39
  182.3 17.1 %maximum_select_fusion.1 = (bf16[1024,3,2,512]{3,0,2,1:T(8,128)(2,1)S(1)}, bf16[1024,3,2,512]{3,0,2,1:T(8,128)(2,1)}) fusion(bf16[1024,3,2,288]{3,0,2,1:T(8,128)(2,1)} %get-tuple-element.39, bf16[1024,3,2,224]{3,0,2,1:T(8,128)(2,1)} %get-tuple-element.41, bf16[1024,3,2,32]{3,0,2,1:T(8,128)(2,1)} %get-tuple-element.35, ...), kind=kLoop, calls=%fused_computation.5 | loop fusion | flops 56623104 | bytes 37749760 | tf_op jit(solution)/shard_map/jit(_where)/select_n | solution.py:60
  216.9 6.5 %subtract_convert_fusion.2 = (bf16[1024,3,1,512]{3,0,2,1:T(8,128)(2,1)}, bf16[1024,3,1,512]{3,0,2,1:T(8,128)(2,1)}) fusion(f32[1024,512]{1,0:T(8,128)S(1)} %get-tuple-element.72, f32[3,512]{1,0:T(4,128)S(1)} %get-tuple-element.127, f32[1024,512]{1,0:T(8,128)S(1)} %get-tuple-element.69, f32[3,512]{1,0:T(4,128)S(1)} %get-tuple-element.124, ...), kind=kLoop, calls=%fused_computation.33 | loop fusion | flops 37748736 | bytes 18911232 | tf_op jit(solution)/shard_map/convert_element_type | solution.py:92
  223.5 7.5 %all-to-all-start.2 = ((f32[16,2,2,8,1024]{4,3,1,2,0:T(8,128)}), f32[16,2,2,8,1024]{4,3,1,2,0:T(8,128)}, u32[]{:S(2)}, u32[]{:S(2)}) async-start(f32[16,2,2,8,1024]{4,3,1,2,0:T(8,128)} %bitcast.500), calls=%async_computation.2 | async-start | bytes 4194304 | tf_op jit(solution)/shard_map/all_to_all | solution.py:39
  230.9 7.3 %fusion.22 = f32[2,2,16,8,1024]{4,3,2,0,1:T(8,128)S(1)} fusion(bf16[1024,3,1,512]{3,0,2,1:T(8,128)(2,1)} %get-tuple-element.17, bf16[1024,3,1,512]{3,0,2,1:T(8,128)(2,1)} %get-tuple-element.16, bf16[1,2,128,3,2,512]{5,2,4,3,1,0:T(8,128)(2,1)} %get-tuple-element.95, bf16[1,2,128,3,2,512]{5,2,4,3,1,0:T(8,128)(2,1)} %get-tuple-element.94), kind=kOutput, calls=%fused_computation.63 | convolution fusion | flops 3240099840 | bytes 11534336 | tf_op jit(solution)/shard_map/qpicrs,jcrs->pqij/dot_general | solution.py:132
  246.4 60.9 %all-to-all-done.2 = f32[16,2,2,8,1024]{4,3,1,2,0:T(8,128)} async-done(((f32[16,2,2,8,1024]{4,3,1,2,0:T(8,128)}), f32[16,2,2,8,1024]{4,3,1,2,0:T(8,128)}, u32[]{:S(2)}, u32[]{:S(2)}) %all-to-all-start.2) | async-done | bytes 2097184 | tf_op jit(solution)/shard_map/all_to_all | solution.py:39
  312.6 8.0 %subtract_convert_fusion.1 = (bf16[1024,3,1,512]{3,0,2,1:T(8,128)(2,1)S(1)}, bf16[1024,3,1,512]{3,0,2,1:T(8,128)(2,1)S(1)}) fusion(f32[1024,512]{1,0:T(8,128)} %get-tuple-element.66, f32[3,512]{1,0:T(4,128)S(1)} %copy-done.21, f32[1024,512]{1,0:T(8,128)} %get-tuple-element.63, f32[3,512]{1,0:T(4,128)S(1)} %copy-done.24, f32[1024,512]{1,0:T(8,128)} %get-tuple-element.67, ...), kind=kLoop, calls=%fused_computation.31 | loop fusion | flops 37748736 | bytes 18911232 | tf_op jit(solution)/shard_map/convert_element_type | solution.py:92
  335.2 5.8 %all-to-all-done.4 = f32[16,2,2,8,1024]{4,3,1,2,0:T(8,128)} async-done(((f32[16,2,2,8,1024]{4,3,1,2,0:T(8,128)}), f32[16,2,2,8,1024]{4,3,1,2,0:T(8,128)}, u32[]{:S(2)}, u32[]{:S(2)}) %all-to-all-start.4) | async-done | bytes 2097184 | tf_op jit(solution)/shard_map/all_to_all | solution.py:39
  341.0 6.2 %all-to-all-start.5 = ((f32[16,2,2,8,1024]{4,3,1,2,0:T(8,128)}), f32[16,2,2,8,1024]{4,3,1,2,0:T(8,128)}, u32[]{:S(2)}, u32[]{:S(2)}) async-start(f32[16,2,2,8,1024]{4,3,1,2,0:T(8,128)} %bitcast.501), calls=%async_computation.5 | async-start | bytes 4194304 | tf_op jit(solution)/shard_map/all_to_all | solution.py:39
  347.2 7.8 %subtract_convert_fusion.3 = (bf16[1024,3,1,512]{3,0,2,1:T(8,128)(2,1)S(1)}, bf16[1024,3,1,512]{3,0,2,1:T(8,128)(2,1)S(1)}) fusion(f32[1024,512]{1,0:T(8,128)} %get-tuple-element.78, f32[3,512]{1,0:T(4,128)S(1)} %bitcast.518, f32[1024,512]{1,0:T(8,128)} %get-tuple-element.161, f32[3,512]{1,0:T(4,128)S(1)} %bitcast.519, f32[1024,512]{1,0:T(8,128)} %get-tuple-element.79, ...), kind=kLoop, calls=%fused_computation.35 | loop fusion | flops 37748736 | bytes 18911232 | tf_op jit(solution)/shard_map/convert_element_type | solution.py:92
  366.3 9.1 %all-to-all-done.5 = f32[16,2,2,8,1024]{4,3,1,2,0:T(8,128)} async-done(((f32[16,2,2,8,1024]{4,3,1,2,0:T(8,128)}), f32[16,2,2,8,1024]{4,3,1,2,0:T(8,128)}, u32[]{:S(2)}, u32[]{:S(2)}) %all-to-all-start.5) | async-done | bytes 2097184 | tf_op jit(solution)/shard_map/all_to_all | solution.py:39
  375.4 5.8 %all-to-all-start.3 = ((f32[16,2,2,8,1024]{4,3,1,2,0:T(8,128)}), f32[16,2,2,8,1024]{4,3,1,2,0:T(8,128)S(1)}, u32[]{:S(2)}, u32[]{:S(2)}) async-start(f32[16,2,2,8,1024]{4,3,1,2,0:T(8,128)} %bitcast.502), calls=%async_computation.3 | async-start | bytes 4194304 | tf_op jit(solution)/shard_map/all_to_all | solution.py:39
  381.3 7.8 %subtract_convert_fusion = (bf16[1024,3,1,512]{3,0,2,1:T(8,128)(2,1)S(1)}, bf16[1024,3,1,512]{3,0,2,1:T(8,128)(2,1)S(1)}) fusion(f32[1024,512]{1,0:T(8,128)} %get-tuple-element.60, f32[3,512]{1,0:T(4,128)S(1)} %copy-done.27, f32[1024,512]{1,0:T(8,128)} %get-tuple-element.158, f32[3,512]{1,0:T(4,128)S(1)} %copy-done.30, f32[1024,512]{1,0:T(8,128)} %get-tuple-element.61, ...), kind=kLoop, calls=%fused_computation.29 | loop fusion | flops 37748736 | bytes 18911232 | tf_op jit(solution)/shard_map/convert_element_type | solution.py:92
  394.0 15.5 %all-to-all-done.3 = f32[16,2,2,8,1024]{4,3,1,2,0:T(8,128)S(1)} async-done(((f32[16,2,2,8,1024]{4,3,1,2,0:T(8,128)}), f32[16,2,2,8,1024]{4,3,1,2,0:T(8,128)S(1)}, u32[]{:S(2)}, u32[]{:S(2)}) %all-to-all-start.3) | async-done | bytes 2097184 | tf_op jit(solution)/shard_map/all_to_all | solution.py:39
  409.5 5.8 %all-to-all-start.6 = ((f32[16,2,2,8,1024]{4,3,1,2,0:T(8,128)}), f32[16,2,2,8,1024]{4,3,1,2,0:T(8,128)}, u32[]{:S(2)}, u32[]{:S(2)}) async-start(f32[16,2,2,8,1024]{4,3,1,2,0:T(8,128)} %bitcast.503), calls=%async_computation.6 | async-start | bytes 4194304 | tf_op jit(solution)/shard_map/all_to_all | solution.py:39
  423.0 20.7 %all-to-all-done.6 = f32[16,2,2,8,1024]{4,3,1,2,0:T(8,128)} async-done(((f32[16,2,2,8,1024]{4,3,1,2,0:T(8,128)}), f32[16,2,2,8,1024]{4,3,1,2,0:T(8,128)}, u32[]{:S(2)}, u32[]{:S(2)}) %all-to-all-start.6) | async-done | bytes 2097184 | tf_op jit(solution)/shard_map/all_to_all | solution.py:39
  (214 shorter events, 123.0 us)
Async XLA Ops:
  4.7 93.6 %all-to-all-start = ((bf16[8,128,3,2,512]{4,1,2,3,0:T(8,128)(2,1)}), bf16[8,128,3,2,512]{4,1,2,3,0:T(8,128)(2,1)}, u32[]{:S(2)}, u32[]{:S(2)}) async-start(bf16[8,128,3,2,512]{4,1,2,3,0:T(8,128)(2,1)} %stack.38), calls=%async_computation | async-start | bytes 12582912 | tf_op jit(solution)/shard_map/all_to_all | solution.py:106
  11.2 50.5 %collective-permute-start.1 = (f32[3,3,2,256]{3,2,1,0:T(2,128)S(1)}, f32[3,3,2,256]{3,2,1,0:T(2,128)S(1)}, u32[]{:S(2)}, u32[]{:S(2)}) collective-permute-start(f32[3,3,2,256]{3,2,1,0:T(2,128)S(1)} %slice_bitcast_fusion.49), channel_id=1, source_target_pairs={{0,1},{1,2},{2,3},{3,4},{4,5},{5,6},{6,7},{7,8},{8,9},{9,10},{10,1... | collective-permute-start | bytes 55304 | tf_op jit(solution)/shard_map/ppermute | solution.py:13
  101.5 37.6 %copy-start = (bf16[8,128,3,2,512]{4,1,0,3,2:T(8,128)(2,1)}, bf16[8,128,3,2,512]{4,1,0,3,2:T(8,128)(2,1)S(1)}, u32[]{:S(2)}) copy-start(bf16[8,128,3,2,512]{4,1,0,3,2:T(8,128)(2,1)S(1)} %copy.34) | copy-start | bytes 18874372
  172.6 50.9 %all-to-all-start.1 = ((f32[16,2,2,8,1024]{4,3,1,2,0:T(8,128)}), f32[16,2,2,8,1024]{4,3,1,2,0:T(8,128)}, u32[]{:S(2)}, u32[]{:S(2)}) async-start(f32[16,2,2,8,1024]{4,3,1,2,0:T(8,128)} %bitcast.499), calls=%async_computation.1 | async-start | bytes 4194304 | tf_op jit(solution)/shard_map/all_to_all | solution.py:39
  211.2 114.4 %collective-permute-start.2 = (bf16[1024,3,2,256]{3,0,2,1:T(8,128)(2,1)}, bf16[1024,3,2,256]{3,0,2,1:T(8,128)(2,1)}, u32[]{:S(2)}, u32[]{:S(2)}) collective-permute-start(bf16[1024,3,2,256]{3,0,2,1:T(8,128)(2,1)} %get-tuple-element.30), channel_id=1, source_target_pairs={{0,1},{1,2},{2,3},{3,4},{4,5},{5,6},{6,7},{7,8},{8,9},{9,10},{10,1... | collective-permute-start | bytes 9437192 | tf_op jit(solution)/shard_map/ppermute | solution.py:23
  214.4 111.2 %collective-permute-start = (bf16[1024,3,2,256]{3,0,2,1:T(8,128)(2,1)}, bf16[1024,3,2,256]{3,0,2,1:T(8,128)(2,1)}, u32[]{:S(2)}, u32[]{:S(2)}) collective-permute-start(bf16[1024,3,2,256]{3,0,2,1:T(8,128)(2,1)} %get-tuple-element.31), channel_id=1, source_target_pairs={{1,0},{2,1},{3,2},{4,3},{5,4},{6,5},{7,6},{8,7},{9,8},{10,9},{11,1... | collective-permute-start | bytes 9437192 | tf_op jit(solution)/shard_map/ppermute | solution.py:25
  223.5 83.9 %all-to-all-start.2 = ((f32[16,2,2,8,1024]{4,3,1,2,0:T(8,128)}), f32[16,2,2,8,1024]{4,3,1,2,0:T(8,128)}, u32[]{:S(2)}, u32[]{:S(2)}) async-start(f32[16,2,2,8,1024]{4,3,1,2,0:T(8,128)} %bitcast.500), calls=%async_computation.2 | async-start | bytes 4194304 | tf_op jit(solution)/shard_map/all_to_all | solution.py:39
  243.5 69.0 %copy-start.20 = (f32[3,512]{1,0:T(4,128)S(1)}, f32[3,512]{1,0:T(4,128)}, u32[]{:S(2)}) copy-start(f32[3,512]{1,0:T(4,128)} %get-tuple-element.120) | copy-start | bytes 18436
  243.5 69.0 %copy-start.21 = (f32[3,512]{1,0:T(4,128)S(1)}, f32[3,512]{1,0:T(4,128)}, u32[]{:S(2)}) copy-start(f32[3,512]{1,0:T(4,128)} %get-tuple-element.121) | copy-start | bytes 18436
  243.5 69.0 %copy-start.22 = (f32[3,512]{1,0:T(4,128)S(1)}, f32[3,512]{1,0:T(4,128)}, u32[]{:S(2)}) copy-start(f32[3,512]{1,0:T(4,128)} %get-tuple-element.122) | copy-start | bytes 18436
  243.5 69.0 %copy-start.23 = (f32[3,512]{1,0:T(4,128)S(1)}, f32[3,512]{1,0:T(4,128)}, u32[]{:S(2)}) copy-start(f32[3,512]{1,0:T(4,128)} %get-tuple-element.117) | copy-start | bytes 18436
  243.6 69.0 %copy-start.24 = (f32[3,512]{1,0:T(4,128)S(1)}, f32[3,512]{1,0:T(4,128)}, u32[]{:S(2)}) copy-start(f32[3,512]{1,0:T(4,128)} %get-tuple-element.118) | copy-start | bytes 18436
  243.6 69.0 %copy-start.25 = (f32[3,512]{1,0:T(4,128)S(1)}, f32[3,512]{1,0:T(4,128)}, u32[]{:S(2)}) copy-start(f32[3,512]{1,0:T(4,128)} %get-tuple-element.119) | copy-start | bytes 18436
  307.3 33.6 %all-to-all-start.4 = ((f32[16,2,2,8,1024]{4,3,1,2,0:T(8,128)}), f32[16,2,2,8,1024]{4,3,1,2,0:T(8,128)}, u32[]{:S(2)}, u32[]{:S(2)}) async-start(f32[16,2,2,8,1024]{4,3,1,2,0:T(8,128)} %bitcast.451), calls=%async_computation.4 | async-start | bytes 4194304 | tf_op jit(solution)/shard_map/all_to_all | solution.py:39
  341.0 34.4 %all-to-all-start.5 = ((f32[16,2,2,8,1024]{4,3,1,2,0:T(8,128)}), f32[16,2,2,8,1024]{4,3,1,2,0:T(8,128)}, u32[]{:S(2)}, u32[]{:S(2)}) async-start(f32[16,2,2,8,1024]{4,3,1,2,0:T(8,128)} %bitcast.501), calls=%async_computation.5 | async-start | bytes 4194304 | tf_op jit(solution)/shard_map/all_to_all | solution.py:39
  361.2 20.0 %copy-start.26 = (f32[3,512]{1,0:T(4,128)S(1)}, f32[3,512]{1,0:T(4,128)}, u32[]{:S(2)}) copy-start(f32[3,512]{1,0:T(4,128)} %get-tuple-element.114) | copy-start | bytes 18436
  361.2 20.0 %copy-start.27 = (f32[3,512]{1,0:T(4,128)S(1)}, f32[3,512]{1,0:T(4,128)}, u32[]{:S(2)}) copy-start(f32[3,512]{1,0:T(4,128)} %get-tuple-element.115) | copy-start | bytes 18436
  361.2 20.0 %copy-start.28 = (f32[3,512]{1,0:T(4,128)S(1)}, f32[3,512]{1,0:T(4,128)}, u32[]{:S(2)}) copy-start(f32[3,512]{1,0:T(4,128)} %get-tuple-element.116) | copy-start | bytes 18436
  361.2 20.0 %copy-start.29 = (f32[3,512]{1,0:T(4,128)S(1)}, f32[3,512]{1,0:T(4,128)}, u32[]{:S(2)}) copy-start(f32[3,512]{1,0:T(4,128)} %get-tuple-element.111) | copy-start | bytes 18436
  361.2 20.0 %copy-start.30 = (f32[3,512]{1,0:T(4,128)S(1)}, f32[3,512]{1,0:T(4,128)}, u32[]{:S(2)}) copy-start(f32[3,512]{1,0:T(4,128)} %get-tuple-element.112) | copy-start | bytes 18436
  361.2 20.0 %copy-start.31 = (f32[3,512]{1,0:T(4,128)S(1)}, f32[3,512]{1,0:T(4,128)}, u32[]{:S(2)}) copy-start(f32[3,512]{1,0:T(4,128)} %get-tuple-element.113) | copy-start | bytes 18436
  375.4 34.1 %all-to-all-start.3 = ((f32[16,2,2,8,1024]{4,3,1,2,0:T(8,128)}), f32[16,2,2,8,1024]{4,3,1,2,0:T(8,128)S(1)}, u32[]{:S(2)}, u32[]{:S(2)}) async-start(f32[16,2,2,8,1024]{4,3,1,2,0:T(8,128)} %bitcast.502), calls=%async_computation.3 | async-start | bytes 4194304 | tf_op jit(solution)/shard_map/all_to_all | solution.py:39
  409.5 34.2 %all-to-all-start.6 = ((f32[16,2,2,8,1024]{4,3,1,2,0:T(8,128)}), f32[16,2,2,8,1024]{4,3,1,2,0:T(8,128)}, u32[]{:S(2)}, u32[]{:S(2)}) async-start(f32[16,2,2,8,1024]{4,3,1,2,0:T(8,128)} %bitcast.503), calls=%async_computation.6 | async-start | bytes 4194304 | tf_op jit(solution)/shard_map/all_to_all | solution.py:39
  418.9 28.0 %copy-start.33 = (s32[6]{0:T(128)S(1)}, s32[6]{0:T(128)}, u32[]{:S(2)}) copy-start(s32[6]{0:T(128)} %param.6) | copy-start | bytes 76
  (28 other events, 283.7 us)
